TPU v7x, 128 devices: a whole 4x4x4 slice. The times are simulated.
128 devices in a mesh: dp: 8 (over z, core), mp: 16 (over y, x).
Axes of the slice: x: 4, y: 4, z: 4, core: 2. Of those that a mesh axis runs over, the one named last changes fastest.
Arguments:
- acts: bfloat16 [1024, 8192], P('dp', 'mp'), may hold values from -6 to 6
- w_up: bfloat16 [8192, 14336], P(None, 'mp'), may hold values from -0.0625 to 0.0625
- out_grad: bfloat16 [1024, 14336], P('dp', 'mp'), may hold values from -6 to 6
- rotation: float32 [8192, 8192], P('mp', 'dp'), may hold values from -6 to 6
Outputs:
- half_rotation: float32 [8192, 8192], P('mp', 'dp')
- next_rotation: float32 [8192, 8192], P('mp', 'dp')
All inputs are finite; a program needn't handle non-finite values.
Results may differ from a plain program's by a relative error of at most 0.017.
Values may be sent and summed in bfloat16 or wider, within the bound.
A program may use at most 128 MiB of HBM per device.

v0:
```python
import functools
import math
import jax
import jax.numpy as jnp
from jax import lax
from jax.sharding import Mesh
from jax.sharding import PartitionSpec as P

D = 8192
ITERS = 2
DP = ("dp_0", "dp_1")
MP = ("mp_0", "mp_1")
DP_MP = ("dp_0", "dp_1", "mp_0", "mp_1")
step_gain = 0.5
epsilon = 1e-06


def by_axis(value, axes):
    return functools.reduce(lax.psum, axes, value)


def in_one_piece(arrays, axis, dim, along):
    both = jnp.concatenate(arrays, axis=along)
    filled, at, gathered = (lax.all_gather(both, axis, axis=dim, tiled=True), 0, [])
    for a in arrays:
        gathered.append(lax.slice_in_dim(filled, at, at + a.shape[along], axis=along))
        at += a.shape[along]
    return tuple(gathered)


def settle(term):
    return lax.optimization_barrier(term.astype(jnp.bfloat16)).astype(jnp.float32)


def contract_cols(left, right):
    return lax.dot_general(
        left, right, (((1,), (1,)), ((), ())), preferred_element_type=jnp.float32
    )


def local(acts, w_up, out_grad, rotation):
    inv_root = D ** (-0.5)
    rot_half = rotation.astype(jnp.bfloat16)
    rot_rows = lax.all_gather(rot_half, DP, axis=1, tiled=True)
    mixed = lax.psum(
        (jnp.dot(acts, rot_rows, preferred_element_type=jnp.float32) * inv_root).astype(
            jnp.bfloat16
        ),
        MP,
    )
    hidden = jnp.dot(mixed, w_up, preferred_element_type=jnp.float32)
    sigmoid_hidden = jax.nn.sigmoid(hidden)
    grad_hidden = (
        out_grad.astype(jnp.float32) * sigmoid_hidden * (1.0 + hidden * (1.0 - sigmoid_hidden))
    ).astype(jnp.bfloat16)
    grad_mixed = lax.psum(contract_cols(grad_hidden, w_up).astype(jnp.bfloat16), MP)
    factor = contract_cols(grad_mixed, rot_rows).astype(jnp.bfloat16)
    act_norm, factor_norm = (
        by_axis(jnp.sum(jnp.square(acts.astype(jnp.float32))), DP_MP),
        by_axis(jnp.sum(jnp.square(factor.astype(jnp.float32))), DP_MP),
    )
    token_count = acts.shape[0] * lax.axis_size(DP)
    spread = (token_count ** (-0.5) + D ** (-0.5)) ** 2
    step_size = (
        step_gain
        * math.sqrt(D)
        / (jnp.sqrt((act_norm + epsilon) * (factor_norm + epsilon)) * spread)
    )
    every_acts, every_factor = in_one_piece((acts, factor), DP, 0, 1)
    groups = lax.axis_size(DP)
    block_rows = acts.shape[0]
    acts_blocks = every_acts.reshape(groups, block_rows, -1)
    factor_blocks = every_factor.reshape(groups, block_rows, -1)
    current = rotation
    first_iterate = rotation
    for iteration in range(ITERS):
        point = (rotation + current).astype(jnp.bfloat16)
        left_sum, right_sum = (
            lax.psum(
                (
                    jnp.dot(every_factor, point, preferred_element_type=jnp.float32) * inv_root
                ).astype(jnp.bfloat16),
                MP,
            ).astype(jnp.float32),
            lax.psum(
                (jnp.dot(every_acts, point, preferred_element_type=jnp.float32) * inv_root).astype(
                    jnp.bfloat16
                ),
                MP,
            ).astype(jnp.float32),
        )
        left = left_sum.astype(jnp.bfloat16).reshape(groups, block_rows, -1)
        right = right_sum.astype(jnp.bfloat16).reshape(groups, block_rows, -1)
        terms = jnp.einsum(
            "ntr,ntc->nrc", acts_blocks, left, preferred_element_type=jnp.float32
        ) - jnp.einsum("ntr,ntc->nrc", factor_blocks, right, preferred_element_type=jnp.float32)
        update = jnp.sum(settle(terms), axis=0)
        current = rotation - step_size * update
        if iteration == 0:
            first_iterate = current
    return (first_iterate, current)


def solution(mesh):
    finer = Mesh(mesh.devices.reshape(4, 2, 4, 4), ("dp_0", "dp_1", "mp_0", "mp_1"))
    placed = (P(DP, MP), P(None, MP), P(DP, MP), P(MP, DP))
    return jax.shard_map(
        local, mesh=finer, in_specs=placed, out_specs=(P(MP, DP), P(MP, DP)), check_vma=False
    )
```

profile of v0, /device:TPU:1, one launch (start us, length us, event | category | flops | bytes accessed | tf_op | source)
XLA Modules:
  0.0 586.6 jit_solution(2937792211861183039)
XLA Ops:
  7.2 2.8 convert_element_type.64
  10.0 0.0 all-reduce.11.cloned.1.call-start
  10.0 53.8 %all-gather.3.cloned.1.call-done = bf16[512,8192]{1,0:T(8,128)(2,1)} async-done(((bf16[512,1024]{1,0:T(8,128)(2,1)}), bf16[512,8192]{1,0:T(8,128)(2,1)}) %all-gather.3.cloned.1.call-update) | async-done | bytes 8388624 | tf_op jit(solution)/shard_map/all_gather | solution.py:44
  63.8 6.0 %fusion = bf16[128,8192]{1,0:T(8,128)(2,1)} fusion(bf16[128,512]{1,0:T(8,128)(2,1)S(1)} %copy-done.7, bf16[512,8192]{1,0:T(8,128)(2,1)} %all-gather.3.cloned.1.call-done), kind=kOutput, calls=%fused_computation.5 | convolution fusion | flops 1075838976 | bytes 10616832 | tf_op jit(solution)/shard_map/dot_general | solution.py:46
  69.9 0.0 all-reduce.13.cloned.1.call-start
  69.9 88.7 %all-reduce.11.cloned.1.call-done = bf16[128,8192]{1,0:T(8,128)(2,1)} async-done(((bf16[128,8192]{1,0:T(8,128)(2,1)}), bf16[128,8192]{1,0:T(8,128)(2,1)}) %all-reduce.11.cloned.1.call-update) | async-done | bytes 2097168 | tf_op jit(solution)/shard_map/psum | solution.py:45
  158.6 20.2 %convolution_convert_fusion = bf16[128,8192]{1,0:T(8,128)(2,1)} fusion(bf16[8192,896]{1,0:T(8,128)(2,1)} %param.5, bf16[128,896]{1,0:T(8,128)(2,1)S(1)} %copy-done.8, bf16[128,8192]{1,0:T(8,128)(2,1)} %all-reduce.11.cloned.1.call-done), kind=kOutput, calls=%fused_computation.6 | convolution fusion | flops 3760291840 | bytes 19103744 | tf_op jit(solution)/shard_map/dot_general | solution.py:36
  178.8 0.0 all-gather.5.cloned.1.call-start
  178.9 89.5 %all-reduce.13.cloned.1.call-done = bf16[128,8192]{1,0:T(8,128)(2,1)} async-done(((bf16[128,8192]{1,0:T(8,128)(2,1)}), bf16[128,8192]{1,0:T(8,128)(2,1)}) %all-reduce.13.cloned.1.call-update) | async-done | bytes 2097168 | tf_op jit(solution)/shard_map/psum | solution.py:56
  268.4 7.7 %multiply_reduce_fusion = (f32[]{:T(128)}, bf16[128,512]{1,0:T(8,128)(2,1)S(1)}) fusion(bf16[128,8192]{1,0:T(8,128)(2,1)} %all-reduce.13.cloned.1.call-done, bf16[512,8192]{1,0:T(8,128)(2,1)} %all-gather.3.cloned.1.call-done), kind=kOutput, calls=%fused_computation.18 | convolution fusion | flops 1074003968 | bytes 10616836 | tf_op jit(solution)/shard_map/dot_general | solution.py:36
  276.1 0.7 pad_maximum_fusion
  276.9 26.4 %all-gather.5.cloned.1.call-done = bf16[1024,1024]{1,0:T(8,128)(2,1)} async-done(((bf16[128,1024]{1,0:T(8,128)(2,1)}), bf16[1024,1024]{1,0:T(8,128)(2,1)}) %all-gather.5.cloned.1.call-update) | async-done | bytes 2097168 | tf_op jit(solution)/shard_map/all_gather | solution.py:24
  303.3 4.0 multiply_convert_fusion.3
  307.2 2.6 multiply_convert_fusion.2
  309.9 0.7 multiply_reduce_fusion.1
  310.6 7.9 %all-reduce.2 = (f32[]{:T(128)}, f32[]{:T(128)}) all-reduce(f32[]{:T(128)} %multiply_reduce_fusion.1, f32[]{:T(128)} %get-tuple-element.18), channel_id=1, replica_groups=mesh['dp_0'=4,'dp_1'=2,'mp_0'=4,'mp_1'=4] {'dp_0'}, use_global_device_ids=true, to_apply=%region_1.0 | all-reduce | flops 2 | bytes 16 | tf_op jit(solution)/shard_map/psum | solution.py:19
  318.5 5.1 all-reduce.3
  323.6 9.9 %all-reduce.1 = (f32[]{:T(128)}, f32[]{:T(128)}) all-reduce(f32[]{:T(128)} %get-tuple-element.8, f32[]{:T(128)} %get-tuple-element.9), channel_id=1, replica_groups=mesh['dp_0'=4,'dp_1'=2,'mp_0'=4,'mp_1'=4] {'mp_0'}, use_global_device_ids=true, to_apply=%region_3.0 | all-reduce | flops 2 | bytes 16 | tf_op jit(solution)/shard_map/psum | solution.py:19
  333.5 9.3 %all-reduce = (f32[]{:T(128)}, f32[]{:T(128)}) all-reduce(f32[]{:T(128)} %get-tuple-element.4, f32[]{:T(128)} %get-tuple-element.5), channel_id=1, replica_groups=mesh['dp_0'=4,'dp_1'=2,'mp_0'=4,'mp_1'=4] {'mp_1'}, use_global_device_ids=true, to_apply=%region_4.0 | all-reduce | flops 2 | bytes 16 | tf_op jit(solution)/shard_map/psum | solution.py:19
  344.2 2.6 fusion.7
  346.9 66.5 %all-reduce.17.cloned.1.call-done = (bf16[8,128,1024]{2,1,0:T(8,128)(2,1)}, bf16[8,128,1024]{2,1,0:T(8,128)(2,1)}) async-done(((bf16[8,128,1024]{2,1,0:T(8,128)(2,1)}, bf16[8,128,1024]{2,1,0:T(8,128)(2,1)}), (bf16[8,128,1024]{2,1,0:T(8,128)(2,1)}, bf16[8,128,1024]{2,1,0:T(8,128)(2,1)})) %all-reduce.17.cloned.1.call-update) | async-done | bytes 4194320 | tf_op jit(solution)/shard_map/psum | solution.py:79
  413.4 9.8 %fusion.10 = f32[8,512,1024]{2,1,0:T(8,128)} fusion(bf16[8,128,512]{2,1,0:T(8,128)(2,1)S(1)} %bitcast.23, bf16[8,128,1024]{2,1,0:T(8,128)(2,1)} %get-tuple-element.12), kind=kOutput, calls=%fused_computation.28 | convolution fusion | flops 1073741824 | bytes 19922944 | tf_op jit(solution)/shard_map/ntr,ntc->nrc/dot_general | solution.py:94
  423.2 11.4 %subtract_convert_fusion.1 = bf16[8,512,1024]{2,1,0:T(8,128)(2,1)} fusion(f32[8,512,1024]{2,1,0:T(8,128)} %fusion.10, bf16[8,128,512]{2,1,0:T(8,128)(2,1)S(1)} %bitcast.25, bf16[8,128,1024]{2,1,0:T(8,128)(2,1)S(1)} %copy-done.3), kind=kOutput, calls=%fused_computation.3 | convolution fusion | flops 1082130432 | bytes 28311552 | tf_op jit(solution)/shard_map/ntr,ntc->nrc/dot_general | solution.py:96
  434.6 5.7 convert_reduce_fusion.1
  440.3 1.8 add_convert_fusion
  442.2 2.6 multiply_convert_fusion
  444.8 2.6 multiply_convert_fusion.1
  447.4 103.4 %all-reduce.15.cloned.1.call-done = (bf16[8,128,1024]{2,1,0:T(8,128)(2,1)}, bf16[8,128,1024]{2,1,0:T(8,128)(2,1)}) async-done(((bf16[8,128,1024]{2,1,0:T(8,128)(2,1)}, bf16[8,128,1024]{2,1,0:T(8,128)(2,1)}), (bf16[8,128,1024]{2,1,0:T(8,128)(2,1)}, bf16[8,128,1024]{2,1,0:T(8,128)(2,1)})) %all-reduce.15.cloned.1.call-update) | async-done | bytes 4194320 | tf_op jit(solution)/shard_map/psum | solution.py:79
  550.8 9.8 %fusion.11 = f32[8,512,1024]{2,1,0:T(8,128)} fusion(bf16[8,128,512]{2,1,0:T(8,128)(2,1)S(1)} %bitcast.24, bf16[8,128,1024]{2,1,0:T(8,128)(2,1)} %get-tuple-element.10), kind=kOutput, calls=%fused_computation.29 | convolution fusion | flops 1073741824 | bytes 19922944 | tf_op jit(solution)/shard_map/ntr,ntc->nrc/dot_general | solution.py:94
  560.7 11.7 %subtract_convert_fusion = bf16[8,512,1024]{2,1,0:T(8,128)(2,1)} fusion(f32[8,512,1024]{2,1,0:T(8,128)} %fusion.11, bf16[8,128,512]{2,1,0:T(8,128)(2,1)S(1)} %bitcast.26, bf16[8,128,1024]{2,1,0:T(8,128)(2,1)S(1)} %copy-done.4), kind=kOutput, calls=%fused_computation.1 | convolution fusion | flops 1082130432 | bytes 28311552 | tf_op jit(solution)/shard_map/ntr,ntc->nrc/dot_general | solution.py:96
  572.3 5.7 convert_reduce_fusion
  578.0 1.8 multiply_subtract_fusion
  (27 shorter events, 0.3 us)
Async XLA Ops:
  7.2 56.7 %copy-start.7 = (bf16[128,512]{1,0:T(8,128)(2,1)S(1)}, bf16[128,512]{1,0:T(8,128)(2,1)}, u32[]{:S(2)}) copy-start(bf16[128,512]{1,0:T(8,128)(2,1)} %param.4) | copy-start | bytes 393220
  7.2 56.7 %all-gather.3.cloned.1.call-start = ((), (), s32[]{:S(2)}) async-start(), calls=%async_computation | async-start | bytes 9437184 | tf_op jit(solution)/shard_map/all_gather | solution.py:44
  10.0 148.6 %all-reduce.11.cloned.1.call-start = ((), (), s32[]{:S(2)}) async-start(), calls=%async_computation.1 | async-start | bytes 4194304 | tf_op jit(solution)/shard_map/psum | solution.py:45
  69.9 88.8 %copy-start.8 = (bf16[128,896]{1,0:T(8,128)(2,1)S(1)}, bf16[128,896]{1,0:T(8,128)(2,1)}, u32[]{:S(2)}) copy-start(bf16[128,896]{1,0:T(8,128)(2,1)} %param.6) | copy-start | bytes 688132
  69.9 198.5 %all-reduce.13.cloned.1.call-start = ((), (), s32[]{:S(2)}) async-start(), calls=%async_computation.2 | async-start | bytes 4194304 | tf_op jit(solution)/shard_map/psum | solution.py:56
  178.8 124.4 %copy-start = (f32[512,1024]{1,0:T(8,128)S(1)}, f32[512,1024]{1,0:T(8,128)}, u32[]{:S(2)}) copy-start(f32[512,1024]{1,0:T(8,128)} %param.7) | copy-start | bytes 6291460
  178.8 124.4 %all-gather.5.cloned.1.call-start = ((), (), s32[]{:S(2)}) async-start(), calls=%async_computation.3 | async-start | bytes 2359296 | tf_op jit(solution)/shard_map/all_gather | solution.py:24
  276.8 136.5 %all-reduce.17.cloned.1.call-start = ((), (), s32[]{:S(2)}) async-start(), calls=%async_computation.5 | async-start | bytes 8388608 | tf_op jit(solution)/shard_map/psum | solution.py:79
  303.3 4.0 copy-start.5
  309.8 241.0 %all-reduce.15.cloned.1.call-start = ((), (), s32[]{:S(2)}) async-start(), calls=%async_computation.4 | async-start | bytes 8388608 | tf_op jit(solution)/shard_map/psum | solution.py:79
  413.4 9.8 %copy-start.1 = (bf16[1024,512]{1,0:T(8,128)(2,1)S(1)}, bf16[1024,512]{1,0:T(8,128)(2,1)}, u32[]{:S(2)}) copy-start(bf16[1024,512]{1,0:T(8,128)(2,1)} %get-tuple-element.16) | copy-start | bytes 3145732
  413.4 9.8 %copy-start.3 = (bf16[8,128,1024]{2,1,0:T(8,128)(2,1)S(1)}, bf16[8,128,1024]{2,1,0:T(8,128)(2,1)}, u32[]{:S(2)}) copy-start(bf16[8,128,1024]{2,1,0:T(8,128)(2,1)} %get-tuple-element.13) | copy-start | bytes 6291460
  440.3 1.9 copy-start.6
  550.8 9.8 %copy-start.2 = (bf16[1024,512]{1,0:T(8,128)(2,1)S(1)}, bf16[1024,512]{1,0:T(8,128)(2,1)}, u32[]{:S(2)}) copy-start(bf16[1024,512]{1,0:T(8,128)(2,1)} %get-tuple-element.16) | copy-start | bytes 3145732
  550.8 9.8 %copy-start.4 = (bf16[8,128,1024]{2,1,0:T(8,128)(2,1)S(1)}, bf16[8,128,1024]{2,1,0:T(8,128)(2,1)}, u32[]{:S(2)}) copy-start(bf16[8,128,1024]{2,1,0:T(8,128)(2,1)} %get-tuple-element.11) | copy-start | bytes 6291460
Sparse Core Ops, SparseCore 0:
  10.3 53.5 all-gather.2
  70.0 88.5 all-reduce.10
  178.9 89.4 all-reduce.12
  276.9 26.2 all-gather.4
  310.0 103.3 all-reduce.16
  447.5 103.2 all-reduce.14
where the time goes:
time: 587 us
  waiting for transfers between devices  428 us (73%)
  matrix products  88.4 us (15%)
  blocking collectives  32.2 us (5%)
  other arithmetic  19.1 us (3%)
  between operations  15.6 us (3%)
    psum x2, waiting for transfers between devices, local(): lax.psum((jnp.dot(every_factor, point, preferred_element_type=jnp.float32...  170 us
    psum x1, waiting for transfers between devices, local(): lax.psum(contract_cols(grad_hidden, w_up).astype(jnp.bfloat16), MP)  89.5 us
    psum x1, waiting for transfers between devices, local(): lax.psum((jnp.dot(acts, rot_rows, preferred_element_type=jnp.float32) * i...  88.7 us
    all_gather x1, waiting for transfers between devices, local(): rot_rows = lax.all_gather(rot_half, DP, axis=1, tiled=True)  53.8 us
    psum x4, blocking collectives, by_axis(): return functools.reduce(lax.psum, axes, value)  32.2 us
    dot_general x2, matrix products, contract_cols(): lax.dot_general(left, right, (((1,), (1,)), ((), ())), preferred_element_...  27.8 us
    all_gather x1, waiting for transfers between devices, in_one_piece(): lax.all_gather(both, axis, axis=dim, tiled=True)  26.4 us
    dot_general x2, matrix products, local(): jnp.einsum('ntr,ntc->nrc', factor_blocks, right, preferred_element_type=j...  23.1 us
  transfers between devices with their start and end apart: 6, of which 6 were waited for; matrix products, arithmetic and copies ran while one was open for 1% of the time, Pallas kernels for 0%

commit v1 on v0

--- a/solution.py
+++ b/solution.py
@@ -13,6 +13,14 @@
 DP_MP = ("dp_0", "dp_1", "mp_0", "mp_1")
 step_gain = 0.5
 epsilon = 1e-06
+
+
+def time_plate_over_axis(sample, axis_key, mesh_dim):
+    b_now = lax.psum(lax.psum(sample, axis_key), mesh_dim)
+    return b_now
+
+
+play_lane = functools.partial(time_plate_over_axis, axis_key="mp_1", mesh_dim="mp_0")
 
 
 def by_axis(value, axes):
@@ -53,7 +61,7 @@
     grad_hidden = (
         out_grad.astype(jnp.float32) * sigmoid_hidden * (1.0 + hidden * (1.0 - sigmoid_hidden))
     ).astype(jnp.bfloat16)
-    grad_mixed = lax.psum(contract_cols(grad_hidden, w_up).astype(jnp.bfloat16), MP)
+    grad_mixed = play_lane(contract_cols(grad_hidden, w_up).astype(jnp.bfloat16))
     factor = contract_cols(grad_mixed, rot_rows).astype(jnp.bfloat16)
     act_norm, factor_norm = (
         by_axis(jnp.sum(jnp.square(acts.astype(jnp.float32))), DP_MP),

time: 587 us -> 617 us (1.051)
  waiting for transfers between devices: 428 us -> 458 us
    psum x1 -> x2, waiting for transfers between devices: 89.5 us -> 120 us  [time_plate_over_axis(): b_now = lax.psum(lax.psum(sample, axis_key), mesh_dim)]
  transfers between devices with their start and end apart: 6 -> 7, of which waited for: 6 -> 7; matrix products, arithmetic and copies ran while one was open for 1% -> 1% of each run, Pallas kernels for 0% -> 0%
where the time goes in v1:
time: 617 us; the launch traced here: 616 us
  waiting for transfers between devices  458 us (74%)
  matrix products  88.4 us (14%)
  blocking collectives  32.2 us (5%)
  other arithmetic  19.1 us (3%)
  between operations  15.6 us (3%)
    psum x2, waiting for transfers between devices, local(): lax.psum((jnp.dot(every_factor, point, preferred_element_type=jnp.float32...  170 us
    psum x2, waiting for transfers between devices, time_plate_over_axis(): b_now = lax.psum(lax.psum(sample, axis_key), mesh_dim)  120 us
    psum x1, waiting for transfers between devices, local(): lax.psum((jnp.dot(acts, rot_rows, preferred_element_type=jnp.float32) * i...  88.7 us
    all_gather x1, waiting for transfers between devices, local(): rot_rows = lax.all_gather(rot_half, DP, axis=1, tiled=True)  53.8 us
    psum x4, blocking collectives, by_axis(): return functools.reduce(lax.psum, axes, value)  32.2 us
    dot_general x2, matrix products, contract_cols(): lax.dot_general(left, right, (((1,), (1,)), ((), ())), preferred_element_...  27.8 us
    all_gather x1, waiting for transfers between devices, in_one_piece(): lax.all_gather(both, axis, axis=dim, tiled=True)  25.7 us
    dot_general x2, matrix products, local(): jnp.einsum('ntr,ntc->nrc', factor_blocks, right, preferred_element_type=j...  23.1 us
  transfers between devices with their start and end apart: 7, of which 7 were waited for; matrix products, arithmetic and copies ran while one was open for 1% of the time, Pallas kernels for 0%

profile of v1, /device:TPU:1, one launch (start us, length us, event | category | flops | bytes accessed | tf_op | source)
XLA Modules:
  0.0 616.4 jit_solution(11206416425595151286)
XLA Ops:
  7.2 2.8 convert_element_type.64
  10.0 0.0 all-reduce.12.cloned.1.call-start
  10.0 53.8 %all-gather.3.cloned.1.call-done = bf16[512,8192]{1,0:T(8,128)(2,1)} async-done(((bf16[512,1024]{1,0:T(8,128)(2,1)}), bf16[512,8192]{1,0:T(8,128)(2,1)}) %all-gather.3.cloned.1.call-update) | async-done | bytes 8388624 | tf_op jit(solution)/shard_map/all_gather | solution.py:52
  63.8 6.0 fusion
  69.9 0.0 all-reduce.14.cloned.1.call-start
  69.9 88.7 %all-reduce.12.cloned.1.call-done = bf16[128,8192]{1,0:T(8,128)(2,1)} async-done(((bf16[128,8192]{1,0:T(8,128)(2,1)}), bf16[128,8192]{1,0:T(8,128)(2,1)}) %all-reduce.12.cloned.1.call-update) | async-done | bytes 2097168 | tf_op jit(solution)/shard_map/psum | solution.py:53
  158.6 20.2 %convolution_convert_fusion = bf16[128,8192]{1,0:T(8,128)(2,1)} fusion(bf16[8192,896]{1,0:T(8,128)(2,1)} %param.5, bf16[128,896]{1,0:T(8,128)(2,1)S(1)} %copy-done.8, bf16[128,8192]{1,0:T(8,128)(2,1)} %all-reduce.12.cloned.1.call-done), kind=kOutput, calls=%fused_computation.6 | convolution fusion | flops 3760291840 | bytes 19103744 | tf_op jit(solution)/shard_map/dot_general | solution.py:44
  178.9 59.3 %all-reduce.14.cloned.1.call-done = bf16[128,8192]{1,0:T(8,128)(2,1)} async-done(((bf16[128,8192]{1,0:T(8,128)(2,1)}), bf16[128,8192]{1,0:T(8,128)(2,1)}) %all-reduce.14.cloned.1.call-update) | async-done | bytes 2097168 | tf_op jit(solution)/shard_map/psum | solution.py:19
  238.2 60.7 %all-reduce.16.cloned.1.call-done = bf16[128,8192]{1,0:T(8,128)(2,1)} async-done(((bf16[128,8192]{1,0:T(8,128)(2,1)}), bf16[128,8192]{1,0:T(8,128)(2,1)}) %all-reduce.16.cloned.1.call-update) | async-done | bytes 2097168 | tf_op jit(solution)/shard_map/psum | solution.py:19
  298.9 7.7 %multiply_reduce_fusion = (f32[]{:T(128)}, bf16[128,512]{1,0:T(8,128)(2,1)S(1)}) fusion(bf16[128,8192]{1,0:T(8,128)(2,1)} %all-reduce.16.cloned.1.call-done, bf16[512,8192]{1,0:T(8,128)(2,1)} %all-gather.3.cloned.1.call-done), kind=kOutput, calls=%fused_computation.18 | convolution fusion | flops 1074003968 | bytes 10616836 | tf_op jit(solution)/shard_map/dot_general | solution.py:44
  306.6 0.7 pad_maximum_fusion
  307.4 25.7 %all-gather.5.cloned.1.call-done = bf16[1024,1024]{1,0:T(8,128)(2,1)} async-done(((bf16[128,1024]{1,0:T(8,128)(2,1)}), bf16[1024,1024]{1,0:T(8,128)(2,1)}) %all-gather.5.cloned.1.call-update) | async-done | bytes 2097168 | tf_op jit(solution)/shard_map/all_gather | solution.py:32
  333.0 4.0 multiply_convert_fusion.3
  337.0 2.6 multiply_convert_fusion.2
  339.7 0.7 multiply_reduce_fusion.1
  340.3 7.9 %all-reduce.2 = (f32[]{:T(128)}, f32[]{:T(128)}) all-reduce(f32[]{:T(128)} %multiply_reduce_fusion.1, f32[]{:T(128)} %get-tuple-element.18), channel_id=1, replica_groups=mesh['dp_0'=4,'dp_1'=2,'mp_0'=4,'mp_1'=4] {'dp_0'}, use_global_device_ids=true, to_apply=%region_1.0 | all-reduce | flops 2 | bytes 16 | tf_op jit(solution)/shard_map/psum | solution.py:27
  348.2 5.1 all-reduce.3
  353.3 9.9 %all-reduce.1 = (f32[]{:T(128)}, f32[]{:T(128)}) all-reduce(f32[]{:T(128)} %get-tuple-element.8, f32[]{:T(128)} %get-tuple-element.9), channel_id=1, replica_groups=mesh['dp_0'=4,'dp_1'=2,'mp_0'=4,'mp_1'=4] {'mp_0'}, use_global_device_ids=true, to_apply=%region_3.0 | all-reduce | flops 2 | bytes 16 | tf_op jit(solution)/shard_map/psum | solution.py:27
  363.2 9.3 %all-reduce = (f32[]{:T(128)}, f32[]{:T(128)}) all-reduce(f32[]{:T(128)} %get-tuple-element.4, f32[]{:T(128)} %get-tuple-element.5), channel_id=1, replica_groups=mesh['dp_0'=4,'dp_1'=2,'mp_0'=4,'mp_1'=4] {'mp_1'}, use_global_device_ids=true, to_apply=%region_4.0 | all-reduce | flops 2 | bytes 16 | tf_op jit(solution)/shard_map/psum | solution.py:27
  374.0 2.6 fusion.7
  376.7 66.5 %all-reduce.20.cloned.1.call-done = (bf16[8,128,1024]{2,1,0:T(8,128)(2,1)}, bf16[8,128,1024]{2,1,0:T(8,128)(2,1)}) async-done(((bf16[8,128,1024]{2,1,0:T(8,128)(2,1)}, bf16[8,128,1024]{2,1,0:T(8,128)(2,1)}), (bf16[8,128,1024]{2,1,0:T(8,128)(2,1)}, bf16[8,128,1024]{2,1,0:T(8,128)(2,1)})) %all-reduce.20.cloned.1.call-update) | async-done | bytes 4194320 | tf_op jit(solution)/shard_map/psum | solution.py:87
  443.1 9.8 %fusion.10 = f32[8,512,1024]{2,1,0:T(8,128)} fusion(bf16[8,128,512]{2,1,0:T(8,128)(2,1)S(1)} %bitcast.23, bf16[8,128,1024]{2,1,0:T(8,128)(2,1)} %get-tuple-element.12), kind=kOutput, calls=%fused_computation.28 | convolution fusion | flops 1073741824 | bytes 19922944 | tf_op jit(solution)/shard_map/ntr,ntc->nrc/dot_general | solution.py:102
  453.0 11.4 %subtract_convert_fusion.1 = bf16[8,512,1024]{2,1,0:T(8,128)(2,1)} fusion(f32[8,512,1024]{2,1,0:T(8,128)} %fusion.10, bf16[8,128,512]{2,1,0:T(8,128)(2,1)S(1)} %bitcast.25, bf16[8,128,1024]{2,1,0:T(8,128)(2,1)S(1)} %copy-done.3), kind=kOutput, calls=%fused_computation.3 | convolution fusion | flops 1082130432 | bytes 28311552 | tf_op jit(solution)/shard_map/ntr,ntc->nrc/dot_general | solution.py:104
  464.4 5.7 convert_reduce_fusion.1
  470.1 1.8 add_convert_fusion
  472.0 2.6 multiply_convert_fusion
  474.6 2.6 multiply_convert_fusion.1
  477.2 103.4 %all-reduce.18.cloned.1.call-done = (bf16[8,128,1024]{2,1,0:T(8,128)(2,1)}, bf16[8,128,1024]{2,1,0:T(8,128)(2,1)}) async-done(((bf16[8,128,1024]{2,1,0:T(8,128)(2,1)}, bf16[8,128,1024]{2,1,0:T(8,128)(2,1)}), (bf16[8,128,1024]{2,1,0:T(8,128)(2,1)}, bf16[8,128,1024]{2,1,0:T(8,128)(2,1)})) %all-reduce.18.cloned.1.call-update) | async-done | bytes 4194320 | tf_op jit(solution)/shard_map/psum | solution.py:87
  580.6 9.8 %fusion.11 = f32[8,512,1024]{2,1,0:T(8,128)} fusion(bf16[8,128,512]{2,1,0:T(8,128)(2,1)S(1)} %bitcast.24, bf16[8,128,1024]{2,1,0:T(8,128)(2,1)} %get-tuple-element.10), kind=kOutput, calls=%fused_computation.29 | convolution fusion | flops 1073741824 | bytes 19922944 | tf_op jit(solution)/shard_map/ntr,ntc->nrc/dot_general | solution.py:102
  590.5 11.7 %subtract_convert_fusion = bf16[8,512,1024]{2,1,0:T(8,128)(2,1)} fusion(f32[8,512,1024]{2,1,0:T(8,128)} %fusion.11, bf16[8,128,512]{2,1,0:T(8,128)(2,1)S(1)} %bitcast.26, bf16[8,128,1024]{2,1,0:T(8,128)(2,1)S(1)} %copy-done.4), kind=kOutput, calls=%fused_computation.1 | convolution fusion | flops 1082130432 | bytes 28311552 | tf_op jit(solution)/shard_map/ntr,ntc->nrc/dot_general | solution.py:104
  602.2 5.7 convert_reduce_fusion
  607.8 1.8 multiply_subtract_fusion
  (30 shorter events, 0.4 us)
Async XLA Ops:
  7.2 56.7 %copy-start.7 = (bf16[128,512]{1,0:T(8,128)(2,1)S(1)}, bf16[128,512]{1,0:T(8,128)(2,1)}, u32[]{:S(2)}) copy-start(bf16[128,512]{1,0:T(8,128)(2,1)} %param.4) | copy-start | bytes 393220
  7.2 56.7 %all-gather.3.cloned.1.call-start = ((), (), s32[]{:S(2)}) async-start(), calls=%async_computation | async-start | bytes 9437184 | tf_op jit(solution)/shard_map/all_gather | solution.py:52
  10.0 148.6 %all-reduce.12.cloned.1.call-start = ((), (), s32[]{:S(2)}) async-start(), calls=%async_computation.1 | async-start | bytes 4194304 | tf_op jit(solution)/shard_map/psum | solution.py:53
  69.9 88.8 %copy-start.8 = (bf16[128,896]{1,0:T(8,128)(2,1)S(1)}, bf16[128,896]{1,0:T(8,128)(2,1)}, u32[]{:S(2)}) copy-start(bf16[128,896]{1,0:T(8,128)(2,1)} %param.6) | copy-start | bytes 688132
  69.9 168.3 %all-reduce.14.cloned.1.call-start = ((), (), s32[]{:S(2)}) async-start(), calls=%async_computation.2 | async-start | bytes 4194304 | tf_op jit(solution)/shard_map/psum | solution.py:19
  178.8 120.1 %all-reduce.16.cloned.1.call-start = ((), (), s32[]{:S(2)}) async-start(), calls=%async_computation.3 | async-start | bytes 4194304 | tf_op jit(solution)/shard_map/psum | solution.py:19
  238.2 94.9 %copy-start = (f32[512,1024]{1,0:T(8,128)S(1)}, f32[512,1024]{1,0:T(8,128)}, u32[]{:S(2)}) copy-start(f32[512,1024]{1,0:T(8,128)} %param.7) | copy-start | bytes 6291460
  238.2 94.9 %all-gather.5.cloned.1.call-start = ((), (), s32[]{:S(2)}) async-start(), calls=%async_computation.4 | async-start | bytes 2359296 | tf_op jit(solution)/shard_map/all_gather | solution.py:32
  307.3 135.8 %all-reduce.20.cloned.1.call-start = ((), (), s32[]{:S(2)}) async-start(), calls=%async_computation.6 | async-start | bytes 8388608 | tf_op jit(solution)/shard_map/psum | solution.py:87
  333.0 4.0 copy-start.5
  339.6 241.0 %all-reduce.18.cloned.1.call-start = ((), (), s32[]{:S(2)}) async-start(), calls=%async_computation.5 | async-start | bytes 8388608 | tf_op jit(solution)/shard_map/psum | solution.py:87
  443.1 9.8 %copy-start.1 = (bf16[1024,512]{1,0:T(8,128)(2,1)S(1)}, bf16[1024,512]{1,0:T(8,128)(2,1)}, u32[]{:S(2)}) copy-start(bf16[1024,512]{1,0:T(8,128)(2,1)} %get-tuple-element.16) | copy-start | bytes 3145732
  443.1 9.8 %copy-start.3 = (bf16[8,128,1024]{2,1,0:T(8,128)(2,1)S(1)}, bf16[8,128,1024]{2,1,0:T(8,128)(2,1)}, u32[]{:S(2)}) copy-start(bf16[8,128,1024]{2,1,0:T(8,128)(2,1)} %get-tuple-element.13) | copy-start | bytes 6291460
  470.1 1.9 copy-start.6
  580.6 9.8 %copy-start.2 = (bf16[1024,512]{1,0:T(8,128)(2,1)S(1)}, bf16[1024,512]{1,0:T(8,128)(2,1)}, u32[]{:S(2)}) copy-start(bf16[1024,512]{1,0:T(8,128)(2,1)} %get-tuple-element.16) | copy-start | bytes 3145732
  580.6 9.8 %copy-start.4 = (bf16[8,128,1024]{2,1,0:T(8,128)(2,1)S(1)}, bf16[8,128,1024]{2,1,0:T(8,128)(2,1)}, u32[]{:S(2)}) copy-start(bf16[8,128,1024]{2,1,0:T(8,128)(2,1)} %get-tuple-element.11) | copy-start | bytes 6291460
Sparse Core Ops, SparseCore 0:
  10.3 53.5 all-gather.2
  70.0 88.5 all-reduce.11
  178.9 59.1 all-reduce.13
  240.3 58.5 all-reduce.15
  307.4 25.5 all-gather.4
  339.7 103.3 all-reduce.19
  477.3 103.2 all-reduce.17
